TPU v7x, 128 devices: a whole 4x4x4 slice. The times are simulated.
128 devices in a mesh: item: 16 (over y, z_lo, core), tbl: 8 (over z_hi, x).
Axes of the slice: x: 4, y: 4, z: 4 (z_hi: 2, z_lo: 2; z = z_hi * 2 + z_lo), core: 2. Of those that a mesh axis runs over, the one named last changes fastest.
Arguments:
- tables: bfloat16 [16, 8192, 128], P('tbl'), may hold values from -2.5 to 2.5
- feat_ids: int32 [131072, 16, 8], P('item', 'tbl'), may hold values from 0 to 8191
- bag_lens: int32 [131072, 16], P('item', 'tbl'), may hold values from 1 to 8
- w_hidden: bfloat16 [2048, 1024], replicated, may hold values from -0.125 to 0.125
- b_hidden: float32 [1024], replicated, may hold values from -3 to 3
- w_out: bfloat16 [1024, 256], replicated, may hold values from -0.1875 to 0.1875
- b_out: float32 [256], replicated, may hold values from -3 to 3
- item_vecs: bfloat16 [4096, 256], P('item'), may hold values from -30 to 30
- elig_mask: int32 [256, 32], P(('item', 'tbl')), may hold values from 0 to 1, as said below
- positives: int32 [131072], P(('item', 'tbl')), may hold values from 0 to 4095, as said below
Outputs:
- user_loss: float32 [131072], P(('item', 'tbl'))
- user_grad: float32 [131072, 256], P(('item', 'tbl'))
- item_grad: float32 [4096, 256], P(('item', 'tbl'))
Inputs may be any that keep to these rules, and one draw needn't show every extreme that they name: Every row of elig_mask holds at least one 1. elig_mask[u // 512, positives[u] // 128] = 1 for every user u.
All inputs are finite; a program needn't handle non-finite values.
Results may differ from a plain program's by a relative error of at most 0.03.
Values may be sent and summed in bfloat16 or wider, within the bound.
No kernel may reach another device: no remote copies, remote signals or barrier semaphores. Data moves between devices by JAX's collectives and lax.ppermute only.
A program may use at most 64 MiB of HBM per device.

v0:
```python
import math

import jax
import jax.numpy as jnp
from jax import lax
from jax.sharding import PartitionSpec as P

IBLK = 128


masked_value = -1e30


def shifted(value, axis, steps):
    count = lax.axis_size(axis)
    pairs = [(source, (source + steps) % count) for source in range(count)]
    return lax.ppermute(value, axis, pairs)


def pool_block(table, block_ids, block_lens):
    gathered = jnp.take(table, block_ids, axis=0).astype(jnp.float32)
    in_bag = jnp.arange(block_ids.shape[1], dtype=jnp.int32)[None, :] < block_lens[:, None]
    return jnp.sum(jnp.where(in_bag[:, :, None], gathered, 0.0), axis=1).astype(jnp.bfloat16)


def visit_first(running, visiting, first_item, queries, positives, eligible):
    maxima, totals, picked = running
    piece_rows = visiting.shape[0]
    block_rows = queries.shape[0] // eligible.shape[0]
    columns = lax.dynamic_slice_in_dim(eligible, first_item // IBLK, piece_rows // IBLK, 1)
    item_index = first_item + jnp.arange(piece_rows, dtype=jnp.int32)
    results = []
    for user_block in range(eligible.shape[0]):
        row_lower = user_block * block_rows
        block_queries = queries[row_lower : row_lower + block_rows]
        wanted = positives[row_lower : row_lower + block_rows]
        previous = (
            maxima[row_lower : row_lower + block_rows],
            totals[row_lower : row_lower + block_rows],
            picked[row_lower : row_lower + block_rows],
        )
        allowed = jnp.repeat(columns[user_block] > 0, IBLK)

        def update(block_queries=block_queries, wanted=wanted, previous=previous, allowed=allowed):
            scores = jnp.einsum(
                "ud,id->ui", block_queries, visiting, preferred_element_type=jnp.float32
            )
            block_max = jnp.max(jnp.where(allowed[None, :], scores, masked_value), axis=1)
            new_max = jnp.maximum(previous[0], block_max)
            summed = previous[1] * jnp.exp(previous[0] - new_max) + jnp.sum(
                jnp.where(allowed[None, :], jnp.exp(scores - new_max[:, None]), 0.0), axis=1
            )
            chosen = previous[2] + jnp.sum(
                jnp.where(item_index[None, :] == wanted[:, None], scores, 0.0), axis=1
            )
            return (new_max, summed, chosen)

        outcome = update()
        results.append(outcome)
    return tuple((jnp.concatenate([result[member] for result in results]) for member in range(3)))


def visit_second(visiting, first_item, queries, positives, eligible, log_norm):
    piece_rows = visiting.shape[0]
    embed_width = visiting.shape[1]
    block_rows = queries.shape[0] // eligible.shape[0]
    columns = lax.dynamic_slice_in_dim(eligible, first_item // IBLK, piece_rows // IBLK, 1)
    item_index = first_item + jnp.arange(piece_rows, dtype=jnp.int32)
    user_terms = []
    item_term = jnp.zeros((piece_rows, embed_width), jnp.float32)
    for user_block in range(eligible.shape[0]):
        row_lower = user_block * block_rows
        block_queries = queries[row_lower : row_lower + block_rows]
        wanted = positives[row_lower : row_lower + block_rows]
        norm_rows = log_norm[row_lower : row_lower + block_rows]
        allowed = jnp.repeat(columns[user_block] > 0, IBLK)

        def contribute(
            block_queries=block_queries, wanted=wanted, norm_rows=norm_rows, allowed=allowed
        ):
            scores = jnp.einsum(
                "ud,id->ui", block_queries, visiting, preferred_element_type=jnp.float32
            )
            probabilities = jnp.where(allowed[None, :], jnp.exp(scores - norm_rows[:, None]), 0.0)
            target = item_index[None, :] == wanted[:, None]
            signal = (probabilities - target.astype(jnp.float32)).astype(jnp.bfloat16)
            user_part = jnp.einsum(
                "ui,id->ud", signal, visiting, preferred_element_type=jnp.float32
            )
            item_part = jnp.einsum(
                "ui,ud->id", signal, block_queries, preferred_element_type=jnp.float32
            )
            return (user_part, item_part)

        user_part, item_part = contribute()
        user_terms.append(user_part)
        item_term = item_term + item_part
    return (jnp.concatenate(user_terms, axis=0), item_term)


def local(
    tables, feat_ids, bag_lens, w_hidden, b_hidden, w_out, b_out, item_vecs, elig_mask, positives
):
    table_shards = lax.axis_size("tbl")
    group_users = feat_ids.shape[0]
    users_here = group_users // table_shards
    pool_rows = math.gcd(group_users, 512)
    pool_count = group_users // pool_rows
    pooled_list = []
    for feature in range(feat_ids.shape[1]):
        feature_ids = feat_ids[:, feature, :].reshape(pool_count, pool_rows, feat_ids.shape[2])
        feature_lens = bag_lens[:, feature].reshape(pool_count, pool_rows)
        table = tables[feature]
        pooled_blocks = lax.map(
            lambda pair, table=table: pool_block(table, pair[0], pair[1]),
            (feature_ids, feature_lens),
        )
        pooled_list.append(pooled_blocks.reshape(group_users, tables.shape[2]))
    pooled = jnp.stack(pooled_list, axis=1).reshape(
        table_shards, users_here, feat_ids.shape[1], tables.shape[2]
    )
    arrived = lax.all_to_all(pooled, "tbl", split_axis=0, concat_axis=2, tiled=True)
    count_users = arrived.shape[1]
    features = arrived.reshape(count_users, arrived.shape[2] * arrived.shape[3])
    hidden = jnp.maximum(
        jnp.dot(features, w_hidden, preferred_element_type=jnp.float32) + b_hidden, 0.0
    ).astype(jnp.bfloat16)
    queries = (jnp.dot(hidden, w_out, preferred_element_type=jnp.float32) + b_out).astype(
        jnp.bfloat16
    )[None][0]
    cycle_size = lax.axis_size("item")
    my_index = lax.axis_index("item")
    item_rows = item_vecs.shape[0]
    users_count = queries.shape[0]
    running = (
        jnp.full((users_count,), masked_value, jnp.float32),
        jnp.zeros((users_count,), jnp.float32),
        jnp.zeros((users_count,), jnp.float32),
    )
    pieces = (item_vecs,)
    directions = (1,)
    offsets = (0,)

    def move_first(moving):
        return (shifted(moving[0], "item", 1),)

    def move_second(moving, carried_grads):
        moved = (shifted(moving[0], "item", 1),)
        grads_moved = (shifted(carried_grads[0], "item", 1),)
        return (moved, grads_moved)

    def first_items(distance):
        return tuple(
            (
                (my_index - direction * distance) % cycle_size * item_rows + offset
                for direction, offset in zip(directions, offsets)
            )
        )

    for visiting, first_item in zip(pieces, first_items(0)):
        running = visit_first(running, visiting, first_item, queries, positives, elig_mask)

    def lap_one(distance, carried):
        moving, running = carried
        moving = move_first(moving)
        for visiting, first_item in zip(moving, first_items(distance)):
            running = visit_first(running, visiting, first_item, queries, positives, elig_mask)
        return (moving, running)

    moving, running = lax.fori_loop(1, cycle_size, lap_one, (pieces, running))
    maxima, totals, picked = running
    log_norm = maxima + jnp.log(totals)
    user_loss = log_norm - picked

    def lap_two(distance, carried):
        moving, grads_moving, user_grad = carried
        new_grads = []
        for visiting, grad_piece, first_item in zip(moving, grads_moving, first_items(distance)):
            user_term, item_term = visit_second(
                visiting, first_item, queries, positives, elig_mask, log_norm
            )
            user_grad = user_grad + user_term
            new_grads.append(grad_piece + item_term)
        moving, grads_moving = move_second(moving, tuple(new_grads))
        return (moving, grads_moving, user_grad)

    start_grads = tuple(
        (jnp.zeros((visiting.shape[0], item_vecs.shape[1]), jnp.float32) for visiting in pieces)
    )
    start_user = jnp.zeros((users_count, item_vecs.shape[1]), jnp.float32)
    moving, grads_moving, user_grad = lax.fori_loop(
        0, cycle_size, lap_two, (pieces, start_grads, start_user)
    )
    item_total = grads_moving[0]
    item_grad = lax.psum_scatter(item_total, "tbl", scatter_dimension=0, tiled=True)
    return (user_loss, user_grad, item_grad)


def solution(mesh):
    in_specs = (
        P("tbl", None, None),
        P("item", "tbl", None),
        P("item", "tbl"),
        P(),
        P(),
        P(),
        P(),
        P("item", None),
        P(("item", "tbl"), None),
        P(("item", "tbl")),
    )
    out_specs = (P(("item", "tbl")), P(("item", "tbl"), None), P(("item", "tbl"), None))
    return jax.shard_map(local, mesh=mesh, in_specs=in_specs, out_specs=out_specs, check_vma=False)
```

profile of v0, /device:TPU:0, one launch (start us, length us, event | category | flops | bytes accessed | tf_op | source)
XLA Modules:
  0.0 1177.0 jit_solution(13827129631512436611)
XLA Ops:
  18.2 356.2 %while.61 = (s32[]{:T(128)}, bf16[16,512,128]{2,1,0:T(8,128)(2,1)}, s32[16,512]{1,0:T(8,128)S(1)}, s32[16,512,8]{2,1,0:T(8,128)}, bf16[8192,128]{1,0:T(8,128)(2,1)}, /*index=5*/s32[]{:T(128)}) while((s32[]{:T(128)}, bf16[16,512,128]{2,1,0:T(8,128)(2,1)}, s32[16,512]{1,0:T(8,128)S(1)}, s32[16,512,8]{2,1,0:T(8,128)}, ...), condition=%wide.region_2.4_spmd, body=%wide.region_0.3_spmd.sunk | while | flops 2064386 | bytes 3676749 | solution.py:114
  19.5 16.2 %gather_fusion = bf16[4096,128]{1,0:T(8,128)(2,1)} fusion(bf16[8192,128]{1,0:T(8,128)(2,1)} %get-tuple-element.930, s32[4096]{0:T(1024)S(1)} %broadcast_clamp_fusion.4), kind=kCustom, calls=%fused_computation.clone.clone.1 | custom fusion | bytes 2113536 | tf_op jit(solution)/shard_map/while/body/eval_jaxpr/jit(_take)/gather | solution.py:21
  41.8 16.2 %gather_fusion = bf16[4096,128]{1,0:T(8,128)(2,1)} fusion(bf16[8192,128]{1,0:T(8,128)(2,1)} %get-tuple-element.930, s32[4096]{0:T(1024)S(1)} %broadcast_clamp_fusion.4), kind=kCustom, calls=%fused_computation.clone.clone.1 | custom fusion | bytes 2113536 | tf_op jit(solution)/shard_map/while/body/eval_jaxpr/jit(_take)/gather | solution.py:21
  64.0 16.2 %gather_fusion = bf16[4096,128]{1,0:T(8,128)(2,1)} fusion(bf16[8192,128]{1,0:T(8,128)(2,1)} %get-tuple-element.930, s32[4096]{0:T(1024)S(1)} %broadcast_clamp_fusion.4), kind=kCustom, calls=%fused_computation.clone.clone.1 | custom fusion | bytes 2113536 | tf_op jit(solution)/shard_map/while/body/eval_jaxpr/jit(_take)/gather | solution.py:21
  86.3 16.2 %gather_fusion = bf16[4096,128]{1,0:T(8,128)(2,1)} fusion(bf16[8192,128]{1,0:T(8,128)(2,1)} %get-tuple-element.930, s32[4096]{0:T(1024)S(1)} %broadcast_clamp_fusion.4), kind=kCustom, calls=%fused_computation.clone.clone.1 | custom fusion | bytes 2113536 | tf_op jit(solution)/shard_map/while/body/eval_jaxpr/jit(_take)/gather | solution.py:21
  108.6 16.2 %gather_fusion = bf16[4096,128]{1,0:T(8,128)(2,1)} fusion(bf16[8192,128]{1,0:T(8,128)(2,1)} %get-tuple-element.930, s32[4096]{0:T(1024)S(1)} %broadcast_clamp_fusion.4), kind=kCustom, calls=%fused_computation.clone.clone.1 | custom fusion | bytes 2113536 | tf_op jit(solution)/shard_map/while/body/eval_jaxpr/jit(_take)/gather | solution.py:21
  130.8 16.2 %gather_fusion = bf16[4096,128]{1,0:T(8,128)(2,1)} fusion(bf16[8192,128]{1,0:T(8,128)(2,1)} %get-tuple-element.930, s32[4096]{0:T(1024)S(1)} %broadcast_clamp_fusion.4), kind=kCustom, calls=%fused_computation.clone.clone.1 | custom fusion | bytes 2113536 | tf_op jit(solution)/shard_map/while/body/eval_jaxpr/jit(_take)/gather | solution.py:21
  153.1 16.2 %gather_fusion = bf16[4096,128]{1,0:T(8,128)(2,1)} fusion(bf16[8192,128]{1,0:T(8,128)(2,1)} %get-tuple-element.930, s32[4096]{0:T(1024)S(1)} %broadcast_clamp_fusion.4), kind=kCustom, calls=%fused_computation.clone.clone.1 | custom fusion | bytes 2113536 | tf_op jit(solution)/shard_map/while/body/eval_jaxpr/jit(_take)/gather | solution.py:21
  175.3 16.2 %gather_fusion = bf16[4096,128]{1,0:T(8,128)(2,1)} fusion(bf16[8192,128]{1,0:T(8,128)(2,1)} %get-tuple-element.930, s32[4096]{0:T(1024)S(1)} %broadcast_clamp_fusion.4), kind=kCustom, calls=%fused_computation.clone.clone.1 | custom fusion | bytes 2113536 | tf_op jit(solution)/shard_map/while/body/eval_jaxpr/jit(_take)/gather | solution.py:21
  197.6 16.2 %gather_fusion = bf16[4096,128]{1,0:T(8,128)(2,1)} fusion(bf16[8192,128]{1,0:T(8,128)(2,1)} %get-tuple-element.930, s32[4096]{0:T(1024)S(1)} %broadcast_clamp_fusion.4), kind=kCustom, calls=%fused_computation.clone.clone.1 | custom fusion | bytes 2113536 | tf_op jit(solution)/shard_map/while/body/eval_jaxpr/jit(_take)/gather | solution.py:21
  219.9 16.2 %gather_fusion = bf16[4096,128]{1,0:T(8,128)(2,1)} fusion(bf16[8192,128]{1,0:T(8,128)(2,1)} %get-tuple-element.930, s32[4096]{0:T(1024)S(1)} %broadcast_clamp_fusion.4), kind=kCustom, calls=%fused_computation.clone.clone.1 | custom fusion | bytes 2113536 | tf_op jit(solution)/shard_map/while/body/eval_jaxpr/jit(_take)/gather | solution.py:21
  242.1 16.2 %gather_fusion = bf16[4096,128]{1,0:T(8,128)(2,1)} fusion(bf16[8192,128]{1,0:T(8,128)(2,1)} %get-tuple-element.930, s32[4096]{0:T(1024)S(1)} %broadcast_clamp_fusion.4), kind=kCustom, calls=%fused_computation.clone.clone.1 | custom fusion | bytes 2113536 | tf_op jit(solution)/shard_map/while/body/eval_jaxpr/jit(_take)/gather | solution.py:21
  264.4 16.2 %gather_fusion = bf16[4096,128]{1,0:T(8,128)(2,1)} fusion(bf16[8192,128]{1,0:T(8,128)(2,1)} %get-tuple-element.930, s32[4096]{0:T(1024)S(1)} %broadcast_clamp_fusion.4), kind=kCustom, calls=%fused_computation.clone.clone.1 | custom fusion | bytes 2113536 | tf_op jit(solution)/shard_map/while/body/eval_jaxpr/jit(_take)/gather | solution.py:21
  286.6 16.2 %gather_fusion = bf16[4096,128]{1,0:T(8,128)(2,1)} fusion(bf16[8192,128]{1,0:T(8,128)(2,1)} %get-tuple-element.930, s32[4096]{0:T(1024)S(1)} %broadcast_clamp_fusion.4), kind=kCustom, calls=%fused_computation.clone.clone.1 | custom fusion | bytes 2113536 | tf_op jit(solution)/shard_map/while/body/eval_jaxpr/jit(_take)/gather | solution.py:21
  308.9 16.2 %gather_fusion = bf16[4096,128]{1,0:T(8,128)(2,1)} fusion(bf16[8192,128]{1,0:T(8,128)(2,1)} %get-tuple-element.930, s32[4096]{0:T(1024)S(1)} %broadcast_clamp_fusion.4), kind=kCustom, calls=%fused_computation.clone.clone.1 | custom fusion | bytes 2113536 | tf_op jit(solution)/shard_map/while/body/eval_jaxpr/jit(_take)/gather | solution.py:21
  331.1 16.2 %gather_fusion = bf16[4096,128]{1,0:T(8,128)(2,1)} fusion(bf16[8192,128]{1,0:T(8,128)(2,1)} %get-tuple-element.930, s32[4096]{0:T(1024)S(1)} %broadcast_clamp_fusion.4), kind=kCustom, calls=%fused_computation.clone.clone.1 | custom fusion | bytes 2113536 | tf_op jit(solution)/shard_map/while/body/eval_jaxpr/jit(_take)/gather | solution.py:21
  353.4 16.2 %gather_fusion = bf16[4096,128]{1,0:T(8,128)(2,1)} fusion(bf16[8192,128]{1,0:T(8,128)(2,1)} %get-tuple-element.930, s32[4096]{0:T(1024)S(1)} %broadcast_clamp_fusion.4), kind=kCustom, calls=%fused_computation.clone.clone.1 | custom fusion | bytes 2113536 | tf_op jit(solution)/shard_map/while/body/eval_jaxpr/jit(_take)/gather | solution.py:21
  378.7 337.2 %while.62 = (s32[]{:T(128)}, bf16[16,512,128]{2,1,0:T(8,128)(2,1)}, s32[16,512]{1,0:T(8,128)S(1)}, s32[16,512,8]{2,1,0:T(8,128)}, bf16[8192,128]{1,0:T(8,128)(2,1)S(1)}, /*index=5*/s32[]{:T(128)}) while((s32[]{:T(128)}, bf16[16,512,128]{2,1,0:T(8,128)(2,1)}, s32[16,512]{1,0:T(8,128)S(1)}, s32[16,512,8]{2,1,0:T(8,128)}, ...), condition=%wide.region_5.7_spmd, body=%wide.region_3.6_spmd.sunk | while | flops 2064386 | bytes 3676749 | solution.py:114
  611.8 15.0 %gather_fusion.1 = bf16[4096,128]{1,0:T(8,128)(2,1)} fusion(bf16[8192,128]{1,0:T(8,128)(2,1)S(1)} %get-tuple-element.912, s32[4096]{0:T(1024)S(1)} %broadcast_clamp_fusion.5), kind=kCustom, calls=%fused_computation.1.clone.clone.1 | custom fusion | bytes 2113536 | tf_op jit(solution)/shard_map/while/body/eval_jaxpr/jit(_take)/gather | solution.py:21
  696.1 15.0 %gather_fusion.1 = bf16[4096,128]{1,0:T(8,128)(2,1)} fusion(bf16[8192,128]{1,0:T(8,128)(2,1)S(1)} %get-tuple-element.912, s32[4096]{0:T(1024)S(1)} %broadcast_clamp_fusion.5), kind=kCustom, calls=%fused_computation.1.clone.clone.1 | custom fusion | bytes 2113536 | tf_op jit(solution)/shard_map/while/body/eval_jaxpr/jit(_take)/gather | solution.py:21
  730.0 49.6 %all-to-all-done = bf16[8,1024,2,128]{3,1,2,0:T(8,128)(2,1)} async-done(((bf16[8,1024,2,128]{3,1,2,0:T(8,128)(2,1)}), bf16[8,1024,2,128]{3,1,2,0:T(8,128)(2,1)}, u32[]{:S(2)}, u32[]{:S(2)}) %all-to-all-start) | async-done | bytes 4194336 | tf_op jit(solution)/shard_map/all_to_all | solution.py:122
  797.9 113.7 %while.63 = (s32[]{:T(128)}, bf16[256,256]{1,0:T(8,128)(2,1)S(1)}, f32[1024]{0:T(1024)S(1)}, f32[1024]{0:T(1024)S(1)}, f32[1024]{0:T(1024)S(1)}, /*index=5*/s32[...) while((s32[]{:T(128)}, bf16[256,256]{1,0:T(8,128)(2,1)S(1)}, ...), condition=%wide.region_19.21_spmd, body=%wide.region_12.20_spmd.sunk | while | flops 136320288 | bytes 3773002 | solution.py:170
  912.3 177.7 %while.64 = (s32[]{:T(128)}, bf16[256,256]{1,0:T(8,128)(2,1)}, f32[256,256]{1,0:T(8,128)S(1)}, f32[1024,256]{1,0:T(8,128)S(1)}, s32[]{:T(128)}, /*index=5*/s32[2...) while((s32[]{:T(128)}, bf16[256,256]{1,0:T(8,128)(2,1)}, ...), condition=%wide.region_21.23_spmd.clone, body=%wide.region_20.22_spmd.clone.sunk | while | flops 405143840 | bytes 10253436 | solution.py:191
  1090.8 79.4 %reduce-scatter.2.cloned.1.call-done = f32[32,256]{1,0:T(8,128)} async-done(((f32[256,256]{1,0:T(8,128)}), f32[32,256]{1,0:T(8,128)}) %reduce-scatter.2.cloned.1.call-update) | async-done | bytes 32784 | tf_op jit(solution)/shard_map/reduce_scatter | solution.py:195
  (801 shorter events, 740.7 us)
Async XLA Ops:
  720.8 58.9 %all-to-all-start = ((bf16[8,1024,2,128]{3,1,2,0:T(8,128)(2,1)}), bf16[8,1024,2,128]{3,1,2,0:T(8,128)(2,1)}, u32[]{:S(2)}, u32[]{:S(2)}) async-start(bf16[8,1024,2,128]{3,1,2,0:T(8,128)(2,1)} %copy.22), calls=%async_computation | async-start | bytes 8388608 | tf_op jit(solution)/shard_map/all_to_all | solution.py:122
  728.6 441.6 %reduce-scatter.2.cloned.1.call-start = ((), (), s32[]{:S(2)}) async-start(), calls=%async_computation.2 | async-start | bytes 294912 | tf_op jit(solution)/shard_map/reduce_scatter | solution.py:195
  913.2 6.6 collective-permute-start.1
  915.3 8.1 collective-permute-start.2
  924.3 6.6 collective-permute-start.1
  926.4 8.1 collective-permute-start.2
  937.5 8.1 collective-permute-start.2
  948.6 8.1 collective-permute-start.2
  957.7 6.6 collective-permute-start.1
  959.7 8.1 collective-permute-start.2
  968.8 6.6 collective-permute-start.1
  970.9 8.1 collective-permute-start.2
  979.9 6.6 collective-permute-start.1
  982.0 8.1 collective-permute-start.2
  991.0 6.6 collective-permute-start.1
  993.1 8.1 collective-permute-start.2
  1004.2 8.1 collective-permute-start.2
  1015.3 8.1 collective-permute-start.2
  1026.4 8.1 collective-permute-start.2
  1037.5 8.1 collective-permute-start.2
  1048.6 8.1 collective-permute-start.2
  1059.7 8.1 collective-permute-start.2
  1070.8 8.1 collective-permute-start.2
  1081.9 8.1 collective-permute-start.2
  (33 other events, 1158.8 us)
Sparse Core Ops, SparseCore 0:
  1090.9 79.2 reduce-scatter.1
where the time goes:
time: 1180 us
  local copies, waits for them, and re-layouts  573 us (49%)
  waiting for transfers between devices  340 us (29%)
  other arithmetic  180 us (15%)
  matrix products  56.9 us (5%)
  between operations  14.2 us (1%)
    gather x32, local copies, waits for them, and re-layouts, pool_block(): gathered = jnp.take(table, block_ids, axis=0).astype(jnp.float32)  500 us
    ppermute x47, waiting for transfers between devices, shifted(): return lax.ppermute(value, axis, pairs)  211 us
    reduce_sum x32, other arithmetic, pool_block(): jnp.sum(jnp.where(in_bag[:, :, None], gathered, 0.0), axis=1)  130 us
    reduce_scatter x1, waiting for transfers between devices, local(): lax.psum_scatter(item_total, 'tbl', scatter_dimension=0, tiled=True)  79.4 us
    all_to_all x1, waiting for transfers between devices, local(): lax.all_to_all(pooled, 'tbl', split_axis=0, concat_axis=2, tiled=True)  49.6 us
    and x32, other arithmetic, pool_block(): gathered = jnp.take(table, block_ids, axis=0).astype(jnp.float32)  35.8 us
  transfers between devices with their start and end apart: 49, of which 49 were waited for; matrix products, arithmetic and copies ran while one was open for 4% of the time, Pallas kernels for 0%

commit v1 on v0

v1 whole, which is shorter than its diff:
```python
import functools

import jax
import jax.numpy as jnp
from jax import lax
from jax.experimental import pallas as pl
from jax.experimental.pallas import tpu as pltpu
from jax.sharding import PartitionSpec as P

IBLK = 128
masked_value = -1e30


def pool_kernel(ids_a, ids_b, tables_ref, out_ref, rows_ref, sums, *, bag, group, tiles):
    table_rows, width = tables_ref.shape[1:]

    @pl.when(pl.program_id(0) == 0)
    def _():
        rows_ref[:table_rows] = tables_ref[0].astype(jnp.float32)
        rows_ref[table_rows : 2 * table_rows] = tables_ref[1].astype(jnp.float32)
        rows_ref[2 * table_rows :] = jnp.zeros((8, width), jnp.float32)

    def pool_tile(ids, feature, tile):
        base = (tile // 16) * (128 * bag) + (tile % 16) * 8
        for user in range(8):
            terms = [
                rows_ref[pl.ds(ids[base + entry * 128 + user], 1), :] for entry in range(bag)
            ]
            while len(terms) > 1:
                terms = [first + second for first, second in zip(terms[::2], terms[1::2])]
            sums[tile, user : user + 1, feature * width : (feature + 1) * width] = terms[0]

    for feature, ids in enumerate((ids_a, ids_b)):

        def step(index, carry, ids=ids, feature=feature):
            for offset in range(tiles):
                pool_tile(ids, feature, index * tiles + offset)
            return carry

        lax.fori_loop(0, group // 8 // tiles, step, 0)
    out_ref[...] = sums[...].reshape(group, 2 * width).astype(jnp.bfloat16)


def pool(tables, ids, users, bag, group=512, tiles=4):
    features, table_rows, width = tables.shape
    steps = users // group
    return pl.pallas_call(
        functools.partial(pool_kernel, bag=bag, group=group, tiles=tiles),
        grid=(steps,),
        in_specs=[
            pl.BlockSpec((group * bag,), lambda i: (i,), memory_space=pltpu.SMEM),
            pl.BlockSpec((group * bag,), lambda i: (i + steps,), memory_space=pltpu.SMEM),
            pl.BlockSpec(tables.shape, lambda i: (0, 0, 0), pipeline_mode=pl.Buffered(1)),
        ],
        out_specs=pl.BlockSpec((group, 2 * width), lambda i: (i, 0)),
        out_shape=jax.ShapeDtypeStruct((users, 2 * width), jnp.bfloat16),
        scratch_shapes=[
            pltpu.VMEM((2 * table_rows + 8, width), jnp.float32),
            pltpu.VMEM((group // 8, 8, 2 * width), jnp.float32),
        ],
        compiler_params=pltpu.CompilerParams(vmem_limit_bytes=40 << 20),
        cost_estimate=pl.CostEstimate(
            flops=users * 2 * bag * width, bytes_accessed=20 << 20, transcendentals=0
        ),
        name="pool",
    )(ids, ids, tables)


def step_kernel(
    arrived_ref, w_hidden_ref, b_hidden_ref, w_out_ref, b_out_ref, items_ref, allowed_ref,
    positives_ref, loss_ref, user_grad_ref, item_grad_ref, scores_ref, *, chunk
):
    sources, users, width = arrived_ref.shape
    items = items_ref.shape[0]
    chunks = items // chunk

    @pl.when(pl.program_id(0) == 0)
    def _():
        item_grad_ref[...] = jnp.zeros_like(item_grad_ref)

    hidden = jnp.dot(
        arrived_ref[0], w_hidden_ref[:width], preferred_element_type=jnp.float32
    )
    for source in range(1, sources):
        hidden += jnp.dot(
            arrived_ref[source],
            w_hidden_ref[source * width : (source + 1) * width],
            preferred_element_type=jnp.float32,
        )
    hidden = jnp.maximum(hidden + b_hidden_ref[...], 0.0).astype(jnp.bfloat16)
    queries = (
        jnp.dot(hidden, w_out_ref[...], preferred_element_type=jnp.float32) + b_out_ref[...]
    ).astype(jnp.bfloat16)

    wanted = positives_ref[...]
    lane = lax.broadcasted_iota(jnp.int32, (users, chunk), 1)

    def fold(value, op):
        pieces = [value[:, k * 128 : (k + 1) * 128] for k in range(chunk // 128)]
        return functools.reduce(op, pieces)

    best = jnp.full((users, 128), masked_value, jnp.float32)
    chosen = jnp.zeros((users, 128), jnp.float32)
    for index in range(chunks):
        span = slice(index * chunk, (index + 1) * chunk)
        scores = lax.dot_general(
            queries, items_ref[span], (((1,), (1,)), ((), ())), preferred_element_type=jnp.float32
        )
        target = lane == wanted - index * chunk
        chosen += fold(jnp.where(target, scores, 0.0), jnp.add)
        scores = jnp.where(allowed_ref[0, :, span] > 0, scores, masked_value)
        best = jnp.maximum(best, fold(scores, jnp.maximum))
        scores_ref[:, span] = scores
    largest = jnp.max(best, axis=1, keepdims=True)
    summed = jnp.zeros((users, 128), jnp.float32)
    for index in range(chunks):
        span = slice(index * chunk, (index + 1) * chunk)
        powers = jnp.exp(scores_ref[:, span] - largest)
        summed += fold(powers, jnp.add)
        scores_ref[:, span] = powers
    total = jnp.sum(summed, axis=1, keepdims=True)
    loss_ref[...] = largest + jnp.log(total) - jnp.sum(chosen, axis=1, keepdims=True)
    scale = 1.0 / total
    user_grad = jnp.zeros(user_grad_ref.shape, jnp.float32)
    for index in range(chunks):
        span = slice(index * chunk, (index + 1) * chunk)
        target = lane == wanted - index * chunk
        signal = (scores_ref[:, span] * scale - jnp.where(target, 1.0, 0.0)).astype(jnp.bfloat16)
        user_grad += jnp.dot(signal, items_ref[span], preferred_element_type=jnp.float32)
        item_grad_ref[span] += lax.dot_general(
            signal, queries, (((0,), (0,)), ((), ())), preferred_element_type=jnp.float32
        )
    user_grad_ref[...] = user_grad


def train_step(arrived, w_hidden, b_hidden, w_out, b_out, items, allowed, positives, tile=256):
    sources, users, width = arrived.shape
    count, embed = items.shape
    hidden = w_hidden.shape[1]
    per_block = users // allowed.shape[0] // tile
    whole = lambda shape: pl.BlockSpec(shape, lambda i: (0,) * len(shape), pipeline_mode=pl.Buffered(1))
    return pl.pallas_call(
        functools.partial(step_kernel, chunk=512),
        grid=(users // tile,),
        in_specs=[
            pl.BlockSpec((sources, tile, width), lambda i: (0, i, 0)),
            whole(w_hidden.shape),
            whole((1, hidden)),
            whole(w_out.shape),
            whole((1, embed)),
            whole(items.shape),
            pl.BlockSpec((1, 1, count), lambda i: (i // per_block, 0, 0)),
            pl.BlockSpec((tile, 1), lambda i: (i, 0)),
        ],
        out_specs=(
            pl.BlockSpec((tile, 1), lambda i: (i, 0)),
            pl.BlockSpec((tile, embed), lambda i: (i, 0)),
            pl.BlockSpec((count, embed), lambda i: (0, 0)),
        ),
        out_shape=(
            jax.ShapeDtypeStruct((users, 1), jnp.float32),
            jax.ShapeDtypeStruct((users, embed), jnp.float32),
            jax.ShapeDtypeStruct((count, embed), jnp.float32),
        ),
        scratch_shapes=[pltpu.VMEM((tile, count), jnp.float32)],
        compiler_params=pltpu.CompilerParams(vmem_limit_bytes=56 << 20),
        cost_estimate=pl.CostEstimate(
            flops=users * (2 * sources * width * hidden + 6 * count * embed),
            bytes_accessed=20 << 20,
            transcendentals=users * count,
        ),
        name="train_step",
    )(
        arrived, w_hidden, b_hidden.reshape(1, -1), w_out, b_out.reshape(1, -1), items,
        allowed[:, None, :], positives[:, None],
    )


def bag_rows(feat_ids, bag_lens, table_rows):
    users, features, bag = feat_ids.shape
    feature = jnp.arange(features, dtype=jnp.int32)[None, :, None]
    counted = jnp.arange(bag, dtype=jnp.int32)[None, None, :] < bag_lens[:, :, None]
    rows = jnp.where(counted, feat_ids + feature * table_rows, features * table_rows)
    rows = rows.transpose(1, 2, 0).reshape(features, bag, users // 128, 128)
    return rows.transpose(0, 2, 1, 3).reshape(-1)


def reduce_items(item_grad):
    rows, embed = item_grad.shape
    item_axis, tbl_axis = lax.axis_size("item"), lax.axis_size("tbl")
    share = rows // item_axis
    pieces = lax.all_to_all(
        item_grad.reshape(item_axis, share, embed), "item", split_axis=0, concat_axis=0
    )
    part = jnp.sum(pieces, axis=0)
    pieces = lax.all_to_all(
        part.reshape(tbl_axis, share // tbl_axis, embed), "tbl", split_axis=0, concat_axis=0
    )
    return jnp.sum(pieces, axis=0)


def local(
    tables, feat_ids, bag_lens, w_hidden, b_hidden, w_out, b_out, item_vecs, elig_mask, positives
):
    table_shards = lax.axis_size("tbl")
    group_users, features, bag = feat_ids.shape
    width = tables.shape[2]
    items = lax.all_gather(item_vecs, "item", axis=0, tiled=True)
    rows = bag_rows(feat_ids, bag_lens, tables.shape[1])
    pooled = pool(tables, rows, group_users, bag)
    pooled = pooled.reshape(table_shards, group_users // table_shards, features * width)
    arrived = lax.all_to_all(pooled, "tbl", split_axis=0, concat_axis=0)
    allowed = jnp.repeat(elig_mask, IBLK, axis=1)
    loss, user_grad, item_part = train_step(
        arrived, w_hidden, b_hidden, w_out, b_out, items, allowed, positives
    )
    return loss[:, 0], user_grad, reduce_items(item_part)


def solution(mesh):
    in_specs = (
        P("tbl", None, None),
        P("item", "tbl", None),
        P("item", "tbl"),
        P(),
        P(),
        P(),
        P(),
        P("item", None),
        P(("item", "tbl"), None),
        P(("item", "tbl")),
    )
    out_specs = (P(("item", "tbl")), P(("item", "tbl"), None), P(("item", "tbl"), None))
    return jax.shard_map(local, mesh=mesh, in_specs=in_specs, out_specs=out_specs, check_vma=False)
```

time: 1180 us -> 313 us (0.27)
  local copies, waits for them, and re-layouts: 573 us -> 5.88 us
  waiting for transfers between devices: 340 us -> 58.6 us
  other arithmetic: 180 us -> 5.84 us
  Pallas kernels: 0 us -> 147 us
  matrix products: 56.9 us -> 0 us
  blocking collectives: 0 us -> 55.3 us
  starting transfers between devices: 9.26 us -> 25.6 us
    gather x32 -> x0, local copies, waits for them, and re-layouts: 500 us -> none  [pool_block(): gathered = jnp.take(table, block_ids, axis=0).astype(jnp.float32)]
    ppermute x47 -> x0, waiting for transfers between devices: 211 us -> none  [shifted(): return lax.ppermute(value, axis, pairs)]
    pallas_call x0 -> x2, Pallas kernels: none -> 147 us  [the longest x1 122 us: pool(): pl.pallas_call(functools.partial(pool_kernel, bag=bag, group=group, tiles...]
    reduce_sum x48 -> x2, other arithmetic: 136 us -> 3.86 us  [the longest x1 3.23 us: reduce_items(): part = jnp.sum(pieces, axis=0)]
    reduce_scatter x1 -> x0, waiting for transfers between devices: 79.4 us -> none  [local(): lax.psum_scatter(item_total, 'tbl', scatter_dimension=0, tiled=True)]
    dot_general x129 -> x0, matrix products: 56.9 us -> none  [the longest x32 20 us: contribute(): jnp.einsum('ui,ud->id', signal, block_queries, preferred_element_type=jnp...]
    all_to_all x0 -> x1, blocking collectives: none -> 55.3 us  [reduce_items(): lax.all_to_all(item_grad.reshape(item_axis, share, embed), 'item', split_...]
    and x32 -> x0, other arithmetic: 35.8 us -> none  [pool_block(): gathered = jnp.take(table, block_ids, axis=0).astype(jnp.float32)]
  transfers between devices with their start and end apart: 49 -> 3, of which waited for: 49 -> 2; matrix products, arithmetic and copies ran while one was open for 4% -> 1% of each run, Pallas kernels for 0% -> 39%
where the time goes in v1:
time: 313 us
  Pallas kernels  147 us (47%)
  waiting for transfers between devices  58.6 us (19%)
  blocking collectives  55.3 us (18%)
  starting transfers between devices  25.6 us (8%)
  between operations  14.1 us (5%)
  local copies, waits for them, and re-layouts  5.88 us (2%)
  other arithmetic  5.84 us (2%)
    pallas_call x1, Pallas kernels, pool(): pl.pallas_call(functools.partial(pool_kernel, bag=bag, group=group, tiles...  122 us
    all_to_all x1, blocking collectives, reduce_items(): lax.all_to_all(item_grad.reshape(item_axis, share, embed), 'item', split_...  55.3 us
    all_to_all x1, waiting for transfers between devices, local(): arrived = lax.all_to_all(pooled, 'tbl', split_axis=0, concat_axis=0)  50 us
    pallas_call x1, Pallas kernels, train_step(): pl.pallas_call(functools.partial(step_kernel, chunk=512), grid=(users //...  25.8 us
    all_to_all x1, starting transfers between devices, reduce_items(): lax.all_to_all(part.reshape(tbl_axis, share // tbl_axis, embed), 'tbl', s...  17.7 us
    all_to_all x1, waiting for transfers between devices, reduce_items(): lax.all_to_all(part.reshape(tbl_axis, share // tbl_axis, embed), 'tbl', s...  7.98 us
    all_to_all x1, starting transfers between devices, local(): arrived = lax.all_to_all(pooled, 'tbl', split_axis=0, concat_axis=0)  7.83 us
  transfers between devices with their start and end apart: 3, of which 2 were waited for; matrix products, arithmetic and copies ran while one was open for 1% of the time, Pallas kernels for 39%

profile of v1, /device:TPU:0, one launch (start us, length us, event | category | flops | bytes accessed | tf_op | source)
XLA Modules:
  0.0 312.6 jit_solution(2471318812339941391)
XLA Ops:
  7.2 0.0 all-gather.2.cloned.1.call-start
  7.2 0.7 all-gather.2.cloned.1.call-update
  7.9 1.2 add_select_fusion
  9.1 0.0 copy-start.1
  9.1 2.2 copy-done.1
  11.3 121.5 %pool.1 = bf16[8192,256]{1,0:T(8,128)(2,1)S(1)} custom-call(s32[131072]{0:T(1024)S(1)} %bitcast.15, s32[131072]{0:T(1024)S(1)} %bitcast.16, bf16[2,8192,128]{2,1,0:T(8,128)(2,1)S(1)} %copy-done.1), custom_call_target="tpu_custom_call" | custom-call | flops 16777216 | bytes 20971520 | tf_op jit(solution)/shard_map/pool/pallas_call | solution.py:47
  132.8 0.0 copy-start
  132.8 2.0 copy-done
  134.8 0.0 copy-start.3
  134.8 0.0 copy-start.4
  134.8 7.8 %all-to-all-start = ((bf16[8,1024,256]{2,1,0:T(8,128)(2,1)}), bf16[8,1024,256]{2,1,0:T(8,128)(2,1)}, u32[]{:S(2)}, u32[]{:S(2)}) async-start(bf16[8,1024,256]{2,1,0:T(8,128)(2,1)} %bitcast.14), calls=%async_computation | async-start | bytes 8388608 | tf_op jit(solution)/shard_map/all_to_all | solution.py:212
  142.6 0.0 copy-done.3
  142.6 1.0 copy.14.positives_ref
  143.6 50.0 %all-to-all-done.arrived_ref = bf16[8,1024,256]{2,1,0:T(8,128)(2,1)} async-done(((bf16[8,1024,256]{2,1,0:T(8,128)(2,1)}), bf16[8,1024,256]{2,1,0:T(8,128)(2,1)}, u32[]{:S(2)}, u32[]{:S(2)}) %all-to-all-start) | async-done | bytes 4194336 | tf_op jit(solution)/shard_map/all_to_all | solution.py:212
  193.6 0.0 copy-done.4
  193.6 0.7 broadcast_in_dim.14
  194.3 25.8 %train_step.1 = (f32[1024,1]{1,0:T(8,128)}, f32[1024,256]{1,0:T(8,128)}, f32[4096,256]{1,0:T(8,128)}) custom-call(bf16[8,1024,256]{2,1,0:T(8,128)(2,1)} %all-to-all-done.arrived_ref, bf16[2048,1024]{1,0:T(8,128)(2,1)} %w_hidden_ref.1, f32[1,1024]{1,0:T(1,128)} %bitcast.20, bf16[1024,256]{1,0:T(8,128)(2,1)} %w_out_ref.1, f32[1,256]{1,0:T(1,128)} %bitcast.21, ...), custom_call_target="tpu_custom_call" | custom-call | flops 10737418240 | bytes 20971520 | tf_op jit(solution)/shard_map/train_step/pallas_call | solution.py:142
  220.1 55.3 %all_to_all.15 = f32[16,256,256]{2,1,0:T(8,128)} all-to-all(f32[16,256,256]{2,1,0:T(8,128)} %bitcast.17), channel_id=1, replica_groups=mesh['item'=16,'tbl'=8] {'item'}, dimensions={0} | all-to-all | bytes 8388608 | tf_op jit(solution)/shard_map/all_to_all | solution.py:192
  275.4 3.2 %reduce_sum.18 = f32[256,256]{1,0:T(8,128)} reduce(f32[16,256,256]{2,1,0:T(8,128)} %all_to_all.15, f32[]{:T(128)} %constant.2.clone.1), dimensions={0}, to_apply=%region_0.1 | reduce | flops 983040 | bytes 4456452 | tf_op jit(solution)/shard_map/reduce_sum | solution.py:195
  278.6 17.7 %all-to-all-start.2 = ((f32[8,32,256]{2,1,0:T(8,128)}), f32[8,32,256]{2,1,0:T(8,128)S(1)}, u32[]{:S(2)}, u32[]{:S(2)}) async-start(f32[8,32,256]{2,1,0:T(8,128)} %bitcast.10), calls=%async_computation.2 | async-start | bytes 524288 | tf_op jit(solution)/shard_map/all_to_all | solution.py:196
  296.3 0.0 copy-done.2
  296.3 0.8 reduce
  297.2 8.0 %all-to-all-done.2 = f32[8,32,256]{2,1,0:T(8,128)S(1)} async-done(((f32[8,32,256]{2,1,0:T(8,128)}), f32[8,32,256]{2,1,0:T(8,128)S(1)}, u32[]{:S(2)}, u32[]{:S(2)}) %all-to-all-start.2) | async-done | bytes 262176 | tf_op jit(solution)/shard_map/all_to_all | solution.py:196
  305.1 0.6 reduce_sum.19
  (3 shorter events, 0.0 us)
Async XLA Ops:
  7.2 186.4 %all-gather.2.cloned.1.call-start = ((), (), s32[]{:S(2)}) async-start(), calls=%async_computation.3 | async-start | bytes 2228224 | tf_op jit(solution)/shard_map/all_gather | solution.py:208
  9.1 2.2 copy-start.1
  132.8 2.0 copy-start
  134.8 7.8 %copy-start.3 = (s32[1024]{0:T(1024)S(1)}, s32[1024]{0:T(1024)}, u32[]{:S(2)}) copy-start(s32[1024]{0:T(1024)} %param.19) | copy-start | bytes 12292
  134.8 58.9 %copy-start.4 = (s32[2,32]{1,0:T(2,128)S(1)}, s32[2,32]{1,0:T(2,128)}, u32[]{:S(2)}) copy-start(s32[2,32]{1,0:T(2,128)} %param.18) | copy-start | bytes 772
  134.8 58.8 %all-to-all-start = ((bf16[8,1024,256]{2,1,0:T(8,128)(2,1)}), bf16[8,1024,256]{2,1,0:T(8,128)(2,1)}, u32[]{:S(2)}, u32[]{:S(2)}) async-start(bf16[8,1024,256]{2,1,0:T(8,128)(2,1)} %bitcast.14), calls=%async_computation | async-start | bytes 8388608 | tf_op jit(solution)/shard_map/all_to_all | solution.py:212
  275.4 20.9 %copy-start.2 = (f32[1024,1]{1,0:T(8,128)S(1)}, f32[1024,1]{1,0:T(8,128)}, u32[]{:S(2)}) copy-start(f32[1024,1]{1,0:T(8,128)} %get-tuple-element.6) | copy-start | bytes 12292
  278.6 26.5 %all-to-all-start.2 = ((f32[8,32,256]{2,1,0:T(8,128)}), f32[8,32,256]{2,1,0:T(8,128)S(1)}, u32[]{:S(2)}, u32[]{:S(2)}) async-start(f32[8,32,256]{2,1,0:T(8,128)} %bitcast.10), calls=%async_computation.2 | async-start | bytes 524288 | tf_op jit(solution)/shard_map/all_to_all | solution.py:196
Sparse Core Ops, SparseCore 0:
  9.7 36.3 all-gather.1

commit v2 on v1

v2 whole, which is shorter than its diff:
```python
import functools

import jax
import jax.numpy as jnp
from jax import lax
from jax.experimental import pallas as pl
from jax.experimental.pallas import tpu as pltpu
from jax.sharding import PartitionSpec as P

IBLK = 128
masked_value = -1e30


def pool_kernel(ids_a, ids_b, tables_ref, out_ref, rows_ref, sums, *, bag, group, tiles):
    table_rows, width = tables_ref.shape[1:]

    @pl.when(pl.program_id(0) == 0)
    def _():
        rows_ref[:table_rows] = tables_ref[0].astype(jnp.float32)
        rows_ref[table_rows : 2 * table_rows] = tables_ref[1].astype(jnp.float32)
        rows_ref[2 * table_rows :] = jnp.zeros((8, width), jnp.float32)

    def pool_tile(ids, feature, tile):
        base = (tile // 16) * (128 * bag) + (tile % 16) * 8
        here = ids.at[pl.ds(base, 128 * (bag - 1) + 8)]
        for user in range(8):
            terms = [
                rows_ref[pl.ds(here[entry * 128 + user], 1), :] for entry in range(bag)
            ]
            while len(terms) > 1:
                terms = [first + second for first, second in zip(terms[::2], terms[1::2])]
            sums[tile, user : user + 1, feature * width : (feature + 1) * width] = terms[0]

    for feature, ids in enumerate((ids_a, ids_b)):

        def step(index, carry, ids=ids, feature=feature):
            for offset in range(tiles):
                pool_tile(ids, feature, index * tiles + offset)
            return carry

        lax.fori_loop(0, group // 8 // tiles, step, 0)
    out_ref[0] = sums[...].reshape(group, 2 * width).astype(jnp.bfloat16)


def pool(tables, ids, owners, users, first, count, bag, group=256, tiles=4):
    features, table_rows, width = tables.shape
    blocks, skip, steps = users // group, first // group, count // group
    place = lambda i: (i // steps) * blocks + skip + i % steps
    return pl.pallas_call(
        functools.partial(pool_kernel, bag=bag, group=group, tiles=tiles),
        grid=(owners * steps,),
        in_specs=[
            pl.BlockSpec((group * bag,), lambda i: (place(i),), memory_space=pltpu.SMEM),
            pl.BlockSpec(
                (group * bag,), lambda i: (place(i) + owners * blocks,), memory_space=pltpu.SMEM
            ),
            pl.BlockSpec(tables.shape, lambda i: (0, 0, 0), pipeline_mode=pl.Buffered(1)),
        ],
        out_specs=pl.BlockSpec((1, group, 2 * width), lambda i: (i // steps, i % steps, 0)),
        out_shape=jax.ShapeDtypeStruct((owners, count, 2 * width), jnp.bfloat16),
        scratch_shapes=[
            pltpu.VMEM((2 * table_rows + 8, width), jnp.float32),
            pltpu.VMEM((group // 8, 8, 2 * width), jnp.float32),
        ],
        compiler_params=pltpu.CompilerParams(vmem_limit_bytes=60 << 20),
        cost_estimate=pl.CostEstimate(
            flops=0, bytes_accessed=owners * count * (64 << 10) // 2, transcendentals=0
        ),
        name="pool",
    )(ids, ids, tables)


def step_kernel(
    core_ref, arrived_ref, w_hidden_ref, b_hidden_ref, w_out_ref, b_out_ref, items_ref, allowed_ref,
    positives_ref, *refs, chunk, resumed
):
    if resumed:
        theirs_in, mine_in = refs[2:4]
        refs = refs[4:]
    loss_ref, user_grad_ref, theirs_ref, mine_ref, scores_ref = refs
    sources, users, width = arrived_ref.shape
    items = items_ref.shape[0]
    half = items // chunk // 2
    core = core_ref[0]

    @pl.when(pl.program_id(0) == 0)
    def _():
        if resumed:
            theirs_ref[...] = theirs_in[...]
            mine_ref[...] = mine_in[...]
        else:
            theirs_ref[...] = jnp.zeros_like(theirs_ref)
            mine_ref[...] = jnp.zeros_like(mine_ref)

    hidden = jnp.dot(
        arrived_ref[0], w_hidden_ref[:width], preferred_element_type=jnp.float32
    )
    for source in range(1, sources):
        hidden += jnp.dot(
            arrived_ref[source],
            w_hidden_ref[source * width : (source + 1) * width],
            preferred_element_type=jnp.float32,
        )
    hidden = jnp.maximum(hidden + b_hidden_ref[...], 0.0).astype(jnp.bfloat16)
    queries = (
        jnp.dot(hidden, w_out_ref[...], preferred_element_type=jnp.float32) + b_out_ref[...]
    ).astype(jnp.bfloat16)

    wanted = positives_ref[...]
    lane = lax.broadcasted_iota(jnp.int32, (users, chunk), 1)

    def fold(value, op):
        pieces = [value[:, k * 128 : (k + 1) * 128] for k in range(chunk // 128)]
        return functools.reduce(op, pieces)

    chunks = []
    for keeper in (1 - core, core):
        for index in range(half):
            first = pl.multiple_of((2 * index + keeper) * chunk, chunk)
            chunks.append((len(chunks), first, items_ref[pl.ds(first, chunk)]))

    best = jnp.full((users, 128), masked_value, jnp.float32)
    chosen = jnp.zeros((users, 128), jnp.float32)
    for index, first, vectors in chunks:
        span = slice(index * chunk, (index + 1) * chunk)
        scores = lax.dot_general(
            queries, vectors, (((1,), (1,)), ((), ())), preferred_element_type=jnp.float32
        )
        target = lane == wanted - first
        chosen += fold(jnp.where(target, scores, 0.0), jnp.add)
        open_here = allowed_ref[0, :, pl.ds(first, chunk)] > 0
        scores = jnp.where(open_here, scores, masked_value)
        best = jnp.maximum(best, fold(scores, jnp.maximum))
        scores_ref[:, span] = scores
    largest = jnp.max(best, axis=1, keepdims=True)
    summed = jnp.zeros((users, 128), jnp.float32)
    for index, _, _ in chunks:
        span = slice(index * chunk, (index + 1) * chunk)
        powers = jnp.exp(scores_ref[:, span] - largest)
        summed += fold(powers, jnp.add)
        scores_ref[:, span] = powers
    total = jnp.sum(summed, axis=1, keepdims=True)
    loss_ref[...] = largest + jnp.log(total) - jnp.sum(chosen, axis=1, keepdims=True)
    scale = 1.0 / total
    user_grad = jnp.zeros(user_grad_ref.shape, jnp.float32)
    for index, first, vectors in chunks:
        span = slice(index * chunk, (index + 1) * chunk)
        target = lane == wanted - first
        signal = (scores_ref[:, span] * scale - jnp.where(target, 1.0, 0.0)).astype(jnp.bfloat16)
        user_grad += jnp.dot(signal, vectors, preferred_element_type=jnp.float32)
        grad_ref = theirs_ref if index < half else mine_ref
        grad_ref[index % half] += lax.dot_general(
            signal, queries, (((0,), (0,)), ((), ())), preferred_element_type=jnp.float32
        )
    user_grad_ref[...] = user_grad


def train_step(
    core, arrived, w_hidden, b_hidden, w_out, b_out, items, allowed, positives, first, before=None,
    tile=256, chunk=256
):
    sources, count, width = arrived.shape
    all_users = positives.shape[0]
    all_items, embed = items.shape
    hidden = w_hidden.shape[1]
    per_block = all_users // allowed.shape[0] // tile
    skip = first // tile
    half = all_items // chunk // 2
    whole = lambda shape: pl.BlockSpec(
        shape, lambda i, core: (0,) * len(shape), pipeline_mode=pl.Buffered(1)
    )
    grads = jax.ShapeDtypeStruct((half, chunk, embed), jnp.float32)
    in_specs = [
        pl.BlockSpec((sources, tile, width), lambda i, core: (0, i, 0)),
        whole(w_hidden.shape),
        whole((1, hidden)),
        whole(w_out.shape),
        whole((1, embed)),
        whole(items.shape),
        pl.BlockSpec((1, 1, all_items), lambda i, core: ((i + skip) // per_block, 0, 0)),
        pl.BlockSpec((tile, 1), lambda i, core: (i + skip, 0)),
    ]
    operands = [
        core, arrived, w_hidden, b_hidden.reshape(1, -1), w_out, b_out.reshape(1, -1), items,
        allowed[:, None, :], positives[:, None],
    ]
    aliases = {}
    if before is not None:
        in_specs += [pl.BlockSpec(memory_space=pl.ANY)] * 2 + [whole(grads.shape)] * 2
        aliases = {len(operands): 0, len(operands) + 1: 1}
        operands += list(before)
    return pl.pallas_call(
        functools.partial(step_kernel, chunk=chunk, resumed=before is not None),
        grid_spec=pltpu.PrefetchScalarGridSpec(
            num_scalar_prefetch=1,
            grid=(count // tile,),
            in_specs=in_specs,
            out_specs=(
                pl.BlockSpec((tile, 1), lambda i, core: (i + skip, 0)),
                pl.BlockSpec((tile, embed), lambda i, core: (i + skip, 0)),
                pl.BlockSpec(grads.shape, lambda i, core: (0, 0, 0)),
                pl.BlockSpec(grads.shape, lambda i, core: (0, 0, 0)),
            ),
            scratch_shapes=[pltpu.VMEM((tile, all_items), jnp.float32)],
        ),
        out_shape=(
            jax.ShapeDtypeStruct((all_users, 1), jnp.float32),
            jax.ShapeDtypeStruct((all_users, embed), jnp.float32),
            grads,
            grads,
        ),
        input_output_aliases=aliases,
        compiler_params=pltpu.CompilerParams(vmem_limit_bytes=60 << 20),
        cost_estimate=pl.CostEstimate(
            flops=count * (2 * sources * width * hidden + 6 * all_items * embed),
            bytes_accessed=20 << 20,
            transcendentals=count * all_items,
        ),
        name="train_step",
    )(*operands)


def bag_rows(feat_ids, bag_lens, table_rows):
    users, features, bag = feat_ids.shape
    feature = jnp.arange(features, dtype=jnp.int32)[None, :, None]
    counted = jnp.arange(bag, dtype=jnp.int32)[None, None, :] < bag_lens[:, :, None]
    rows = jnp.where(counted, feat_ids + feature * table_rows, features * table_rows)
    rows = rows.transpose(1, 2, 0).reshape(features, bag, users // 128, 128)
    return rows.transpose(0, 2, 1, 3).reshape(-1)


def reduce_items(theirs, mine):
    cores, members = 2, lax.axis_size("item")
    pairs = [(member, member ^ 1) for member in range(members)]
    part = mine + lax.ppermute(theirs, "item", pairs)
    same_core = [list(range(core, members, cores)) for core in range(cores)]
    pieces = lax.all_to_all(
        part, "item", split_axis=0, concat_axis=0, axis_index_groups=same_core
    )
    part = jnp.sum(pieces, axis=0)
    share, embed = part.shape
    shards = lax.axis_size("tbl")
    pieces = lax.all_to_all(
        part.reshape(shards, share // shards, embed), "tbl", split_axis=0, concat_axis=0
    )
    return jnp.sum(pieces, axis=0)


SPLIT = (768, 256)


def local(
    tables, feat_ids, bag_lens, w_hidden, b_hidden, w_out, b_out, item_vecs, elig_mask, positives
):
    owners = lax.axis_size("tbl")
    bag = feat_ids.shape[2]
    users = positives.shape[0]
    core = (lax.axis_index("item") % 2).reshape(1)
    items = lax.all_gather(item_vecs, "item", axis=0, tiled=True)
    rows = bag_rows(feat_ids, bag_lens, tables.shape[1])
    allowed = jnp.repeat(elig_mask, IBLK, axis=1)
    parts, first = [], 0
    for count in SPLIT:
        pooled = pool(tables, rows, owners, users, first, count, bag)
        parts.append((first, lax.all_to_all(pooled, "tbl", split_axis=0, concat_axis=0)))
        first += count
    outcome = None
    for first, arrived in parts:
        outcome = train_step(
            core, arrived, w_hidden, b_hidden, w_out, b_out, items, allowed, positives, first, outcome
        )
    loss, user_grad, theirs, mine = outcome
    return loss[:, 0], user_grad, reduce_items(theirs, mine)


def solution(mesh):
    in_specs = (
        P("tbl", None, None),
        P("item", "tbl", None),
        P("item", "tbl"),
        P(),
        P(),
        P(),
        P(),
        P("item", None),
        P(("item", "tbl"), None),
        P(("item", "tbl")),
    )
    out_specs = (P(("item", "tbl")), P(("item", "tbl"), None), P(("item", "tbl"), None))
    return jax.shard_map(local, mesh=mesh, in_specs=in_specs, out_specs=out_specs, check_vma=False)
```

time: 313 us -> 263 us (0.84)
  waiting for transfers between devices: 58.6 us -> 19.1 us
  blocking collectives: 55.3 us -> 31.6 us
  Pallas kernels: 147 us -> 159 us
    all_to_all x2 -> x3, waiting for transfers between devices: 58 us -> 14 us  [the longest x1 7.98 us: reduce_items(): lax.all_to_all(part.reshape(shards, share // shards, embed), 'tbl', split...]
    all_to_all x1, blocking collectives: 55.3 us -> 31.6 us  [reduce_items(): lax.all_to_all(part, 'item', split_axis=0, concat_axis=0, axis_index_grou...]
    pallas_call x1 -> x2, Pallas kernels: 122 us -> 128 us  [pool(): pl.pallas_call(functools.partial(pool_kernel, bag=bag, group=group, tiles...]
    pallas_call x1 -> x2, Pallas kernels: 25.8 us -> 31.5 us  [train_step(): pl.pallas_call(functools.partial(step_kernel, chunk=chunk, resumed=before...]
    ppermute x0 -> x1, waiting for transfers between devices: none -> 4.37 us  [reduce_items(): part = mine + lax.ppermute(theirs, 'item', pairs)]
    all_to_all x2 -> x3, starting transfers between devices: 25.5 us -> 27.5 us  [the longest x2 19.6 us: local(): lax.all_to_all(pooled, 'tbl', split_axis=0, concat_axis=0)]
  transfers between devices with their start and end apart: 3 -> 5, of which waited for: 2 -> 3; matrix products, arithmetic and copies ran while one was open for 1% -> 2% of each run, Pallas kernels for 39% -> 56%
where the time goes in v2:
time: 263 us; the launch traced here: 262 us
  Pallas kernels  159 us (60%)
  blocking collectives  31.6 us (12%)
  starting transfers between devices  27.5 us (10%)
  waiting for transfers between devices  19.1 us (7%)
  between operations  14.1 us (5%)
  other arithmetic  6.23 us (2%)
  local copies, waits for them, and re-layouts  4.35 us (2%)
    pallas_call x2, Pallas kernels, pool(): pl.pallas_call(functools.partial(pool_kernel, bag=bag, group=group, tiles...  128 us
    all_to_all x1, blocking collectives, reduce_items(): lax.all_to_all(part, 'item', split_axis=0, concat_axis=0, axis_index_grou...  31.6 us
    pallas_call x2, Pallas kernels, train_step(): pl.pallas_call(functools.partial(step_kernel, chunk=chunk, resumed=before...  31.5 us
    all_to_all x2, starting transfers between devices, local(): lax.all_to_all(pooled, 'tbl', split_axis=0, concat_axis=0)  19.6 us
    all_to_all x1, waiting for transfers between devices, reduce_items(): lax.all_to_all(part.reshape(shards, share // shards, embed), 'tbl', split...  7.98 us
    all_to_all x1, starting transfers between devices, reduce_items(): lax.all_to_all(part.reshape(shards, share // shards, embed), 'tbl', split...  7.83 us
    all_to_all x2, waiting for transfers between devices, local(): lax.all_to_all(pooled, 'tbl', split_axis=0, concat_axis=0)  6.05 us
  transfers between devices with their start and end apart: 5, of which 3 were waited for; matrix products, arithmetic and copies ran while one was open for 2% of the time, Pallas kernels for 56%

profile of v2, /device:TPU:0, one launch (start us, length us, event | category | flops | bytes accessed | tf_op | source)
XLA Modules:
  0.0 262.2 jit_solution(6624443134866752800)
XLA Ops:
  7.2 0.0 all-gather.2.cloned.1.call-start
  7.2 0.7 all-gather.2.cloned.1.call-update
  7.9 2.0 add_select_fusion
  9.9 94.3 %pool.3 = bf16[8,768,256]{2,1,0:T(8,128)(2,1)} custom-call(s32[131072]{0:T(1024)} %bitcast.13, s32[131072]{0:T(1024)} %bitcast.14, bf16[2,8192,128]{2,1,0:T(8,128)(2,1)} %tables_ref.3), custom_call_target="tpu_custom_call" | custom-call | bytes 201326592 | tf_op jit(solution)/shard_map/pool/pallas_call | solution.py:49
  104.1 7.7 %all-to-all-start.1 = ((bf16[8,768,256]{2,1,0:T(8,128)(2,1)}), bf16[8,768,256]{2,1,0:T(8,128)(2,1)S(1)}, u32[]{:S(2)}, u32[]{:S(2)}) async-start(bf16[8,768,256]{2,1,0:T(8,128)(2,1)} %pool.3), calls=%async_computation.1 | async-start | bytes 6291456 | tf_op jit(solution)/shard_map/all_to_all | solution.py:265
  111.8 33.6 %pool.2 = bf16[8,256,256]{2,1,0:T(8,128)(2,1)} custom-call(s32[131072]{0:T(1024)} %bitcast.15, s32[131072]{0:T(1024)} %bitcast.16, bf16[2,8192,128]{2,1,0:T(8,128)(2,1)} %tables_ref.3), custom_call_target="tpu_custom_call" | custom-call | bytes 67108864 | tf_op jit(solution)/shard_map/pool/pallas_call | solution.py:49
  145.5 6.0 %all-to-all-done.1.arrived_ref = bf16[8,768,256]{2,1,0:T(8,128)(2,1)S(1)} async-done(((bf16[8,768,256]{2,1,0:T(8,128)(2,1)}), bf16[8,768,256]{2,1,0:T(8,128)(2,1)S(1)}, u32[]{:S(2)}, u32[]{:S(2)}) %all-to-all-start.1) | async-done | bytes 3145760 | tf_op jit(solution)/shard_map/all_to_all | solution.py:265
  151.5 1.6 copy-done.1
  153.2 11.9 %all-to-all-start = ((bf16[8,256,256]{2,1,0:T(8,128)(2,1)}), bf16[8,256,256]{2,1,0:T(8,128)(2,1)S(1)}, u32[]{:S(2)}, u32[]{:S(2)}) async-start(bf16[8,256,256]{2,1,0:T(8,128)(2,1)} %pool.2), calls=%async_computation | async-start | bytes 2097152 | tf_op jit(solution)/shard_map/all_to_all | solution.py:265
  165.1 1.0 copy.18.positives_ref
  166.1 0.7 broadcast_in_dim.15
  166.8 20.0 %train_step.2 = (f32[1024,1]{1,0:T(8,128)}, f32[1024,256]{1,0:T(8,128)}, f32[8,256,256]{2,1,0:T(8,128)}, f32[8,256,256]{2,1,0:T(8,128)}) custom-call(s32[1]{0:T(128)} %bitcast.core_ref, bf16[8,768,256]{2,1,0:T(8,128)(2,1)} %copy-done.1, bf16[2048,1024]{1,0:T(8,128)(2,1)} %w_hidden_ref.3, f32[1,1024]{1,0:T(1,128)} %bitcast.20, bf16[1024,256]{1,0:T(8,128)(2,1)} %w_out_ref.3, ...), custom_call_target="tpu_custom_call" | custom-call | flops 8053063680 | bytes 20971520 | tf_op jit(solution)/shard_map/train_step/pallas_call | solution.py:192
  186.8 0.0 all-to-all-done.arrived_ref
  186.9 1.0 copy-done
  187.8 11.5 %train_step.3 = (f32[1024,1]{1,0:T(8,128)}, f32[1024,256]{1,0:T(8,128)}, f32[8,256,256]{2,1,0:T(8,128)}, f32[8,256,256]{2,1,0:T(8,128)}) custom-call(s32[1]{0:T(128)} %bitcast.core_ref, bf16[8,256,256]{2,1,0:T(8,128)(2,1)} %copy-done, bf16[2048,1024]{1,0:T(8,128)(2,1)} %w_hidden_ref.3, ...), custom_call_target="tpu_custom_call", output_to_operand_aliasing={{0}: (9, {}), {1}: (10, {})} | custom-call | flops 2684354560 | bytes 20971520 | tf_op jit(solution)/shard_map/train_step/pallas_call | solution.py:192
  199.3 0.0 collective-permute-start
  199.4 4.4 %collective-permute-done = f32[8,256,256]{2,1,0:T(8,128)S(1)} collective-permute-done((f32[8,256,256]{2,1,0:T(8,128)}, f32[8,256,256]{2,1,0:T(8,128)S(1)}, u32[]{:S(2)}, u32[]{:S(2)}) %collective-permute-start) | collective-permute-done | bytes 2097184 | tf_op jit(solution)/shard_map/ppermute | solution.py:235
  203.7 2.0 add.18
  205.7 31.6 %all_to_all.20 = f32[8,256,256]{2,1,0:T(8,128)S(1)} all-to-all(f32[8,256,256]{2,1,0:T(8,128)S(1)} %add.18), channel_id=1, replica_groups={{0,16,32,48,64,80,96,112},{8,24,40,56,72,88,104,120},{1,17,33,49,65,81,..., dimensions={0} | all-to-all | bytes 4194304 | tf_op jit(solution)/shard_map/all_to_all | solution.py:237
  237.3 0.8 reduce_sum.18
  238.1 7.8 %all-to-all-start.3 = ((f32[8,32,256]{2,1,0:T(8,128)}), f32[8,32,256]{2,1,0:T(8,128)S(1)}, u32[]{:S(2)}, u32[]{:S(2)}) async-start(f32[8,32,256]{2,1,0:T(8,128)} %bitcast.12), calls=%async_computation.3 | async-start | bytes 524288 | tf_op jit(solution)/shard_map/all_to_all | solution.py:243
  246.0 0.8 reduce
  246.8 8.0 %all-to-all-done.3 = f32[8,32,256]{2,1,0:T(8,128)S(1)} async-done(((f32[8,32,256]{2,1,0:T(8,128)}), f32[8,32,256]{2,1,0:T(8,128)S(1)}, u32[]{:S(2)}, u32[]{:S(2)}) %all-to-all-start.3) | async-done | bytes 262176 | tf_op jit(solution)/shard_map/all_to_all | solution.py:243
  254.8 0.6 reduce_sum.19
  (10 shorter events, 0.0 us)
Async XLA Ops:
  7.2 159.0 %all-gather.2.cloned.1.call-start = ((), (), s32[]{:S(2)}) async-start(), calls=%async_computation.4 | async-start | bytes 2228224 | tf_op jit(solution)/shard_map/all_gather | solution.py:259
  104.1 47.4 %all-to-all-start.1 = ((bf16[8,768,256]{2,1,0:T(8,128)(2,1)}), bf16[8,768,256]{2,1,0:T(8,128)(2,1)S(1)}, u32[]{:S(2)}, u32[]{:S(2)}) async-start(bf16[8,768,256]{2,1,0:T(8,128)(2,1)} %pool.3), calls=%async_computation.1 | async-start | bytes 6291456 | tf_op jit(solution)/shard_map/all_to_all | solution.py:265
  145.5 19.6 %copy-start.3 = (s32[1024]{0:T(1024)S(1)}, s32[1024]{0:T(1024)}, u32[]{:S(2)}) copy-start(s32[1024]{0:T(1024)} %param.19) | copy-start | bytes 12292
  145.5 20.7 %copy-start.4 = (s32[2,32]{1,0:T(2,128)S(1)}, s32[2,32]{1,0:T(2,128)}, u32[]{:S(2)}) copy-start(s32[2,32]{1,0:T(2,128)} %param.18) | copy-start | bytes 772
  151.5 1.6 copy-start.1
  153.2 33.7 %all-to-all-start = ((bf16[8,256,256]{2,1,0:T(8,128)(2,1)}), bf16[8,256,256]{2,1,0:T(8,128)(2,1)S(1)}, u32[]{:S(2)}, u32[]{:S(2)}) async-start(bf16[8,256,256]{2,1,0:T(8,128)(2,1)} %pool.2), calls=%async_computation | async-start | bytes 2097152 | tf_op jit(solution)/shard_map/all_to_all | solution.py:265
  186.8 1.0 copy-start
  199.3 4.4 %collective-permute-start = (f32[8,256,256]{2,1,0:T(8,128)}, f32[8,256,256]{2,1,0:T(8,128)S(1)}, u32[]{:S(2)}, u32[]{:S(2)}) collective-permute-start(f32[8,256,256]{2,1,0:T(8,128)} %get-tuple-element.18), channel_id=1, source_target_pairs={{0,8},{8,0},{16,24},{24,16},{32,40},{40,32},{48,56},{56,48},{64,72... | collective-permute-start | bytes 6291464 | tf_op jit(solution)/shard_map/ppermute | solution.py:235
  237.3 8.7 %copy-start.2 = (f32[1024,1]{1,0:T(8,128)S(1)}, f32[1024,1]{1,0:T(8,128)}, u32[]{:S(2)}) copy-start(f32[1024,1]{1,0:T(8,128)} %get-tuple-element.15) | copy-start | bytes 12292
  238.1 16.6 %all-to-all-start.3 = ((f32[8,32,256]{2,1,0:T(8,128)}), f32[8,32,256]{2,1,0:T(8,128)S(1)}, u32[]{:S(2)}, u32[]{:S(2)}) async-start(f32[8,32,256]{2,1,0:T(8,128)} %bitcast.12), calls=%async_computation.3 | async-start | bytes 524288 | tf_op jit(solution)/shard_map/all_to_all | solution.py:243
Sparse Core Ops, SparseCore 0:
  9.7 36.3 all-gather.1
